TPU v7x, 32 devices: a whole 2x2x4 slice. The times are simulated.
32 devices in a mesh: pulse: 4 (over z), tile: 8 (over y, x, core).
Axes of the slice: x: 2, y: 2, z: 4, core: 2. Of those that a mesh axis runs over, the one named last changes fastest.
Arguments:
- raw: bfloat16 [2, 128, 2048], P(None, ('pulse', 'tile')), may hold values from -6 to 6
- filt: bfloat16 [2, 1024, 2048], replicated, may hold values from -0.125 to 0.125
- range_off: int32 [128], P(('pulse', 'tile')), may hold values from 0 to 1024
- fine: int32 [128], P(('pulse', 'tile')), may hold values from 0 to 3
- dop: int32 [128], P(('pulse', 'tile')), may hold values from 0 to 511
- pulse_order: int32 [32, 4], P(('pulse', 'tile')), may hold values from 0 to 3, each once within a row
- band_idx: int32 [8, 128], P(None, ('pulse', 'tile')), may hold values from 0 to 1023
Outputs:
- image: bfloat16 [2, 512, 32768], P(None, 'pulse', 'tile')
Inputs may be any that keep to these rules, and one draw needn't show every extreme that they name: `pulse_order`: each row is a permutation of 0 .. 3.
All inputs are finite; a program needn't handle non-finite values.
Results may differ from a plain program's by a relative error of at most 0.0065.
Values may be sent and summed in bfloat16 or wider, within the bound.
A program may use at most 192 MiB of HBM per device.

v0:
```python
import jax
import jax.numpy as jnp
from jax import lax
from jax.sharding import PartitionSpec as P

BAND = 1024
STEPS = 4
PS = 1
R_DEV = 128


def compress(windows, filt):
    wr = windows[:, 0]
    wi = windows[:, 1]
    prof_re = jnp.dot(wr, filt[0], preferred_element_type=jnp.float32) - jnp.dot(
        wi, filt[1], preferred_element_type=jnp.float32
    )
    prof_im = jnp.dot(wr, filt[1], preferred_element_type=jnp.float32) + jnp.dot(
        wi, filt[0], preferred_element_type=jnp.float32
    )
    return jnp.stack([prof_re, prof_im], 1).astype(jnp.bfloat16)


def cut_band(profile, start):
    segment = lax.dynamic_slice_in_dim(profile, start, BAND + 1, 1)
    return (segment[:, :BAND], segment[:, BAND])


def interpolate(pieces, edges, shifts):
    first = pieces.astype(jnp.float32)
    second = jnp.concatenate([first[..., 1:], edges.astype(jnp.float32)[..., None]], -1)
    first = jnp.repeat(first, 4, axis=-1)
    second = jnp.repeat(second, 4, axis=-1)
    phase_q = (jnp.arange(4 * BAND, dtype=jnp.int32) % 4).astype(jnp.float32)
    weight = (4.0 * phase_q[None, :] + shifts.astype(jnp.float32)[:, None]) / 16.0
    weight = weight[:, None, :]
    return first * (1.0 - weight) + second * weight


def gradient_terms(samples, summed):
    sr = samples[:, 0]
    si = samples[:, 1]
    g_re = jnp.sum(sr * summed[None, 0] + si * summed[None, 1], axis=-1)
    g_im = jnp.sum(si * summed[None, 0] - sr * summed[None, 1], axis=-1)
    return (g_re, g_im)


def shards(raw, filt, range_off, fine, dop, pulse_order, band_idx):
    n_pulse = lax.axis_size("pulse")
    n_tile = lax.axis_size("tile")
    devices = n_pulse * n_tile
    pulse_index = lax.axis_index("pulse")
    p_dev = raw.shape[1]
    win = filt.shape[1]
    pulses = p_dev * devices
    total_rows = R_DEV * n_pulse
    cols = 4 * BAND
    all_order, all_dop, all_fine = (
        lax.all_gather(pulse_order, ("pulse", "tile"), axis=0, tiled=True),
        lax.all_gather(dop, ("pulse", "tile"), axis=0, tiled=True),
        lax.all_gather(fine, ("pulse", "tile"), axis=0, tiled=True),
    )
    owners = jnp.arange(devices, dtype=jnp.int32)[:, None] * p_dev
    rows_here = pulse_index * R_DEV + jnp.arange(R_DEV, dtype=jnp.int32)
    accumulated = jnp.zeros((2, R_DEV, cols), jnp.float32)
    for step in range(STEPS):
        local_sel = pulse_order[0, step * PS : (step + 1) * PS]
        picked = jnp.take(raw, local_sel, axis=1)
        offsets = jnp.take(range_off, local_sel)
        windows = jax.vmap(
            lambda row, off: lax.dynamic_slice_in_dim(row, off, win, 1), in_axes=(1, 0)
        )(picked, offsets)
        profile = compress(windows, filt)
        chosen = (owners + all_order[:, step * PS : (step + 1) * PS]).reshape(-1)
        starts = jnp.take(band_idx, local_sel, axis=1)
        pieces, edges = jax.vmap(jax.vmap(cut_band, in_axes=(0, 0)), in_axes=(None, 0))(
            profile, starts
        )
        pieces = pieces.reshape(n_tile * PS, 2, BAND)
        edges = edges.reshape(n_tile * PS, 2)
        mine_pieces, mine_edges = (
            lax.all_to_all(pieces, "tile", split_axis=0, concat_axis=0, tiled=True),
            lax.all_to_all(edges, "tile", split_axis=0, concat_axis=0, tiled=True),
        )
        pieces, edges = (
            lax.all_gather(mine_pieces, "pulse", axis=0, tiled=True),
            lax.all_gather(mine_edges, "pulse", axis=0, tiled=True),
        )
        shifts = jnp.take(all_fine, chosen)
        samples = interpolate(pieces, edges, shifts)
        summed = jnp.sum(samples, axis=0)
        g_re, g_im = gradient_terms(samples, summed)
        g_re, g_im = lax.psum((g_re, g_im), "tile")
        scale = jnp.sqrt(g_re * g_re + g_im * g_im + 1.0)
        c_re = (g_re / scale)[:, None]
        c_im = (-g_im / scale)[:, None]
        sr = samples[:, 0]
        si = samples[:, 1]
        right = jnp.concatenate([c_re * sr - c_im * si, c_re * si + c_im * sr], 0).astype(
            jnp.bfloat16
        )
        dops = jnp.take(all_dop, chosen)
        angle = (
            2.0
            * jnp.pi
            * (dops[:, None] * rows_here[None, :] % total_rows).astype(jnp.float32)
            / total_rows
        )
        norm_scale = jnp.sqrt(jnp.float32(pulses))
        e_re = (jnp.cos(angle) / norm_scale).astype(jnp.bfloat16)
        e_im = (jnp.sin(angle) / norm_scale).astype(jnp.bfloat16)
        left = jnp.stack([jnp.concatenate([e_re, -e_im], 0), jnp.concatenate([e_im, e_re], 0)], 0)
        accumulated = accumulated + jnp.einsum(
            "zkr,kc->zrc", left, right, preferred_element_type=jnp.float32
        )
    return accumulated.astype(jnp.bfloat16)


def solution(mesh):
    return jax.shard_map(
        shards,
        mesh=mesh,
        in_specs=(
            P(None, ("pulse", "tile"), None),
            P(),
            P(("pulse", "tile")),
            P(("pulse", "tile")),
            P(("pulse", "tile")),
            P(("pulse", "tile"), None),
            P(None, ("pulse", "tile")),
        ),
        out_specs=P(None, "pulse", "tile"),
        check_vma=False,
    )
```

profile of v0, /device:TPU:0, one launch (start us, length us, event | category | flops | bytes accessed | tf_op | source)
XLA Modules:
  0.0 478.1 jit_solution(11086329522314578801)
XLA Ops:
  21.8 10.7 %while.17 = (s32[]{:T(128)}, bf16[1,2,2048]{2,1,0:T(2,128)(2,1)S(1)}, s32[8,3]{0,1:T(4,128)S(1)}, bf16[8,2,1025]{2,1,0:T(2,128)(2,1)S(1)}, s32[]{:T(128)}) while((s32[]{:T(128)}, bf16[1,2,2048]{2,1,0:T(2,128)(2,1)S(1)}, s32[8,3]{0,1:T(4,128)S(1)}, bf16[8,2,1025]{2,1,0:T(2,128)(2,1)S(1)}, s32[]{:T(128)}) %tuple.191), condition=%wide.while_cond.13, body=%wide.while_body.13.sunk | while | flops 2 | bytes 9321 | solution.py:25
  33.3 5.2 %all-to-all-start.7 = ((bf16[8,1,2]{2,1,0:T(2,128)(2,1)}), bf16[8,1,2]{2,1,0:T(2,128)(2,1)S(1)}, u32[]{:S(2)}, u32[]{:S(2)}) async-start(bf16[8,1,2]{2,1,0:T(2,128)(2,1)} %copy.117), calls=%async_computation.7 | async-start | bytes 8192 | tf_op jit(solution)/shard_map/all_to_all | solution.py:83
  39.1 42.3 %all-gather.4 = s32[32,1,4]{2,1,0:T(1,128)S(1)} all-gather(s32[1,1,4]{2,1,0:T(1,128)S(1)} %bitcast.332), channel_id=1, replica_groups=mesh['pulse'=4,'tile'=8] {'pulse','tile'}, dimensions={0}, use_global_device_ids=true | all-gather | bytes 528 | tf_op jit(solution)/shard_map/all_gather | solution.py:59
  82.0 37.2 %all-reduce.6 = (s32[128]{0:T(128)S(1)}, s32[128]{0:T(128)S(1)}) all-reduce(s32[128]{0:T(128)S(1)} %dynamic-update-slice.19, s32[128]{0:T(128)S(1)} %dynamic-update-slice.18), channel_id=1, replica_groups=mesh['pulse'=4,'tile'=8] {'pulse','tile'}, use_global_device_ids=true, to_apply=%add.5 | all-reduce | flops 256 | bytes 2048
  136.4 10.9 %while.16 = (s32[]{:T(128)}, bf16[1,2,2048]{2,1,0:T(2,128)(2,1)S(1)}, s32[8,3]{0,1:T(4,128)S(1)}, bf16[8,2,1025]{2,1,0:T(2,128)(2,1)S(1)}, s32[]{:T(128)}) while((s32[]{:T(128)}, bf16[1,2,2048]{2,1,0:T(2,128)(2,1)S(1)}, s32[8,3]{0,1:T(4,128)S(1)}, bf16[8,2,1025]{2,1,0:T(2,128)(2,1)S(1)}, s32[]{:T(128)}) %tuple.188), condition=%wide.while_cond.10, body=%wide.while_body.10.sunk | while | flops 2 | bytes 9321 | solution.py:25
  159.4 11.5 %while.15 = (s32[]{:T(128)}, bf16[1,2,2048]{2,1,0:T(2,128)(2,1)S(1)}, s32[8,3]{0,1:T(4,128)S(1)}, bf16[8,2,1025]{2,1,0:T(2,128)(2,1)S(1)}, s32[]{:T(128)}) while((s32[]{:T(128)}, bf16[1,2,2048]{2,1,0:T(2,128)(2,1)S(1)}, s32[8,3]{0,1:T(4,128)S(1)}, bf16[8,2,1025]{2,1,0:T(2,128)(2,1)S(1)}, s32[]{:T(128)}) %tuple.185), condition=%wide.while_cond.7, body=%wide.while_body.7.sunk | while | flops 2 | bytes 9321 | solution.py:25
  183.1 11.3 %while.14 = (s32[]{:T(128)}, bf16[1,2,2048]{2,1,0:T(2,128)(2,1)S(1)}, s32[8,3]{0,1:T(4,128)S(1)}, bf16[8,2,1025]{2,1,0:T(2,128)(2,1)S(1)}, s32[]{:T(128)}) while((s32[]{:T(128)}, bf16[1,2,2048]{2,1,0:T(2,128)(2,1)S(1)}, s32[8,3]{0,1:T(4,128)S(1)}, bf16[8,2,1025]{2,1,0:T(2,128)(2,1)S(1)}, s32[]{:T(128)}) %tuple.182), condition=%wide.while_cond.4, body=%wide.while_body.4.sunk | while | flops 2 | bytes 9321 | solution.py:25
  219.4 15.0 %all-to-all-start.5 = ((bf16[8,1,2]{2,1,0:T(2,128)(2,1)}), bf16[8,1,2]{2,1,0:T(2,128)(2,1)S(1)}, u32[]{:S(2)}, u32[]{:S(2)}) async-start(bf16[8,1,2]{2,1,0:T(2,128)(2,1)} %copy.107), calls=%async_computation.5 | async-start | bytes 8192 | tf_op jit(solution)/shard_map/all_to_all | solution.py:83
  234.4 13.8 %all-gather.3 = bf16[32,1,2]{2,1,0:T(2,128)(2,1)S(1)} all-gather(bf16[8,1,2]{2,1,0:T(2,128)(2,1)S(1)} %all-to-all-done.7), channel_id=5, replica_groups=mesh['pulse'=4,'tile'=8] {'pulse'}, dimensions={0}, use_global_device_ids=true | all-gather | bytes 160 | tf_op jit(solution)/shard_map/all_gather | solution.py:87
  248.3 4.1 all-to-all-start.3
  252.4 13.2 %all-gather.2 = bf16[32,1,2]{2,1,0:T(2,128)(2,1)S(1)} all-gather(bf16[8,1,2]{2,1,0:T(2,128)(2,1)S(1)} %all-to-all-done.5), channel_id=4, replica_groups=mesh['pulse'=4,'tile'=8] {'pulse'}, dimensions={0}, use_global_device_ids=true | all-gather | bytes 160 | tf_op jit(solution)/shard_map/all_gather | solution.py:87
  265.7 4.2 all-to-all-start.1
  269.9 13.2 %all-gather.1 = bf16[32,1,2]{2,1,0:T(2,128)(2,1)S(1)} all-gather(bf16[8,1,2]{2,1,0:T(2,128)(2,1)S(1)} %all-to-all-done.3), channel_id=3, replica_groups=mesh['pulse'=4,'tile'=8] {'pulse'}, dimensions={0}, use_global_device_ids=true | all-gather | bytes 160 | tf_op jit(solution)/shard_map/all_gather | solution.py:87
  283.2 4.2 all-to-all-start.6
  287.4 13.2 %all-gather = bf16[32,1,2]{2,1,0:T(2,128)(2,1)S(1)} all-gather(bf16[8,1,2]{2,1,0:T(2,128)(2,1)S(1)} %all-to-all-done.1), channel_id=2, replica_groups=mesh['pulse'=4,'tile'=8] {'pulse'}, dimensions={0}, use_global_device_ids=true | all-gather | bytes 160 | tf_op jit(solution)/shard_map/all_gather | solution.py:87
  301.1 4.2 all-to-all-start.4
  305.3 13.4 %all_gather.42 = bf16[32,2,1024]{2,1,0:T(2,128)(2,1)S(1)} all-gather(bf16[8,2,1024]{2,1,0:T(2,128)(2,1)S(1)} %all-to-all-done.6), channel_id=1, replica_groups=mesh['pulse'=4,'tile'=8] {'pulse'}, dimensions={0}, use_global_device_ids=true | all-gather | bytes 163840 | tf_op jit(solution)/shard_map/all_gather | solution.py:86
  320.1 4.2 all-to-all-start.2
  324.3 13.4 %all_gather.40 = bf16[32,2,1024]{2,1,0:T(2,128)(2,1)S(1)} all-gather(bf16[8,2,1024]{2,1,0:T(2,128)(2,1)S(1)} %all-to-all-done.4), channel_id=1, replica_groups=mesh['pulse'=4,'tile'=8] {'pulse'}, dimensions={0}, use_global_device_ids=true | all-gather | bytes 163840 | tf_op jit(solution)/shard_map/all_gather | solution.py:86
  339.8 4.2 all-to-all-start
  344.0 13.4 %all_gather.38 = bf16[32,2,1024]{2,1,0:T(2,128)(2,1)S(1)} all-gather(bf16[8,2,1024]{2,1,0:T(2,128)(2,1)S(1)} %all-to-all-done.2), channel_id=1, replica_groups=mesh['pulse'=4,'tile'=8] {'pulse'}, dimensions={0}, use_global_device_ids=true | all-gather | bytes 163840 | tf_op jit(solution)/shard_map/all_gather | solution.py:86
  358.5 13.6 %all_gather.35 = bf16[32,2,1024]{2,1,0:T(2,128)(2,1)S(1)} all-gather(bf16[8,2,1024]{2,1,0:T(2,128)(2,1)S(1)} %all-to-all-done), channel_id=1, replica_groups=mesh['pulse'=4,'tile'=8] {'pulse'}, dimensions={0}, use_global_device_ids=true | all-gather | bytes 163840 | tf_op jit(solution)/shard_map/all_gather | solution.py:86
  376.4 3.6 copy.121
  380.0 3.9 broadcast_in_dim.159
  387.6 5.1 %add_reduce_fusion = f32[2,1024,4]{2,1,0:T(8,128)S(1)} fusion(f32[32,1024,4]{0,2,1:T(4,128)} %copy.123, f32[32,1024,4]{0,2,1:T(4,128)} %copy.122, f32[32,2,1024]{0,2,1:T(8,128)S(1)} %copy.120, f32[32,2,1024]{0,2,1:T(8,128)} %copy.114), kind=kLoop, calls=%fused_computation.52 | loop fusion | flops 1040384 | bytes 1605632 | tf_op jit(solution)/shard_map/reduce_sum | solution.py:91
  398.6 3.6 copy.111
  402.3 3.9 broadcast_in_dim.152
  409.8 5.1 %add_reduce_fusion.1 = f32[2,1024,4]{2,1,0:T(8,128)S(1)} fusion(f32[32,1024,4]{0,2,1:T(4,128)} %copy.113, f32[32,1024,4]{0,2,1:T(4,128)} %copy.112, f32[32,2,1024]{0,2,1:T(8,128)S(1)} %copy.110, f32[32,2,1024]{0,2,1:T(8,128)} %copy.104), kind=kLoop, calls=%fused_computation.53 | loop fusion | flops 1040384 | bytes 1605632 | tf_op jit(solution)/shard_map/reduce_sum | solution.py:91
  429.6 5.1 %add_reduce_fusion.2 = f32[2,1024,4]{2,1,0:T(8,128)S(1)} fusion(f32[32,1024,4]{0,2,1:T(4,128)} %copy.103, f32[32,1024,4]{0,2,1:T(4,128)} %copy.102, f32[32,2,1024]{0,2,1:T(8,128)S(1)} %copy.100, f32[32,2,1024]{0,2,1:T(8,128)S(1)} %copy.94), kind=kLoop, calls=%fused_computation.54 | loop fusion | flops 1040384 | bytes 1605632 | tf_op jit(solution)/shard_map/reduce_sum | solution.py:91
  435.9 5.0 %add_reduce_fusion.3 = f32[2,1024,4]{2,1,0:T(8,128)S(1)} fusion(f32[32,1024,4]{0,2,1:T(4,128)} %copy.93, f32[32,1024,4]{0,2,1:T(4,128)} %copy.92, f32[32,2,1024]{0,2,1:T(8,128)S(1)} %copy.90, f32[32,2,1024]{0,2,1:T(8,128)S(1)} %copy.84), kind=kLoop, calls=%fused_computation.55 | loop fusion | flops 1040384 | bytes 1605632 | tf_op jit(solution)/shard_map/reduce_sum | solution.py:91
  450.5 3.7 copy.85
  459.4 12.1 %all-reduce.7 = (f32[32]{0:T(128)S(1)}, f32[32]{0:T(128)S(1)}, f32[32]{0:T(128)S(1)}, f32[32]{0:T(128)S(1)}, f32[32]{0:T(128)S(1)}, /*index=5*/f32[32]{0:T(128)S(1)}, f32[32]{0:T(128)S(1)}, f32[32]{0:T(128)S(1)}) all-reduce(f32[32]{0:T(128)S(1)} %get-tuple-element.157, ...), channel_id=1, replica_groups=mesh['pulse'=4,'tile'=8] {'tile'}, use_global_device_ids=true, to_apply=%region_4.8 | all-reduce | flops 256 | bytes 2048 | tf_op jit(solution)/shard_map/psum | solution.py:93
  (334 shorter events, 184.0 us)
Async XLA Ops:
  13.9 6.3 %copy-start = (bf16[2,1024,2048]{2,1,0:T(8,128)(2,1)S(1)}, bf16[2,1024,2048]{2,1,0:T(8,128)(2,1)}, u32[]{:S(2)}) copy-start(bf16[2,1024,2048]{2,1,0:T(8,128)(2,1)} %param.14) | copy-start | bytes 25165828
  20.3 18.9 %copy-start.24 = (s32[1,4]{1,0:T(1,128)S(1)}, s32[1,4]{1,0:T(1,128)}, u32[]{:S(2)}) copy-start(s32[1,4]{1,0:T(1,128)} %param.18) | copy-start | bytes 52
  20.3 61.2 %copy-start.26 = (s32[4]{0:T(128)S(1)}, s32[4]{0:T(128)}, u32[]{:S(2)}) copy-start(s32[4]{0:T(128)} %param.17) | copy-start | bytes 52
  20.3 61.5 %copy-start.27 = (s32[4]{0:T(128)S(1)}, s32[4]{0:T(128)}, u32[]{:S(2)}) copy-start(s32[4]{0:T(128)} %param.16) | copy-start | bytes 52
  33.3 186.1 %all-to-all-start.7 = ((bf16[8,1,2]{2,1,0:T(2,128)(2,1)}), bf16[8,1,2]{2,1,0:T(2,128)(2,1)S(1)}, u32[]{:S(2)}, u32[]{:S(2)}) async-start(bf16[8,1,2]{2,1,0:T(2,128)(2,1)} %copy.117), calls=%async_computation.7 | async-start | bytes 8192 | tf_op jit(solution)/shard_map/all_to_all | solution.py:83
  219.4 28.9 %all-to-all-start.5 = ((bf16[8,1,2]{2,1,0:T(2,128)(2,1)}), bf16[8,1,2]{2,1,0:T(2,128)(2,1)S(1)}, u32[]{:S(2)}, u32[]{:S(2)}) async-start(bf16[8,1,2]{2,1,0:T(2,128)(2,1)} %copy.107), calls=%async_computation.5 | async-start | bytes 8192 | tf_op jit(solution)/shard_map/all_to_all | solution.py:83
  248.3 17.4 %all-to-all-start.3 = ((bf16[8,1,2]{2,1,0:T(2,128)(2,1)}), bf16[8,1,2]{2,1,0:T(2,128)(2,1)S(1)}, u32[]{:S(2)}, u32[]{:S(2)}) async-start(bf16[8,1,2]{2,1,0:T(2,128)(2,1)} %copy.97), calls=%async_computation.3 | async-start | bytes 8192 | tf_op jit(solution)/shard_map/all_to_all | solution.py:83
  265.7 17.5 %all-to-all-start.1 = ((bf16[8,1,2]{2,1,0:T(2,128)(2,1)}), bf16[8,1,2]{2,1,0:T(2,128)(2,1)S(1)}, u32[]{:S(2)}, u32[]{:S(2)}) async-start(bf16[8,1,2]{2,1,0:T(2,128)(2,1)} %copy.87), calls=%async_computation.1 | async-start | bytes 8192 | tf_op jit(solution)/shard_map/all_to_all | solution.py:83
  283.2 17.9 %all-to-all-start.6 = ((bf16[8,2,1024]{2,1,0:T(2,128)(2,1)}), bf16[8,2,1024]{2,1,0:T(2,128)(2,1)S(1)}, u32[]{:S(2)}, u32[]{:S(2)}) async-start(bf16[8,2,1024]{2,1,0:T(2,128)(2,1)} %slice_bitcast_fusion.8), calls=%async_computation.6 | async-start | bytes 65536 | tf_op jit(solution)/shard_map/all_to_all | solution.py:82
  301.1 19.0 %all-to-all-start.4 = ((bf16[8,2,1024]{2,1,0:T(2,128)(2,1)}), bf16[8,2,1024]{2,1,0:T(2,128)(2,1)S(1)}, u32[]{:S(2)}, u32[]{:S(2)}) async-start(bf16[8,2,1024]{2,1,0:T(2,128)(2,1)} %slice_bitcast_fusion.9), calls=%async_computation.4 | async-start | bytes 65536 | tf_op jit(solution)/shard_map/all_to_all | solution.py:82
  320.1 19.7 %all-to-all-start.2 = ((bf16[8,2,1024]{2,1,0:T(2,128)(2,1)}), bf16[8,2,1024]{2,1,0:T(2,128)(2,1)S(1)}, u32[]{:S(2)}, u32[]{:S(2)}) async-start(bf16[8,2,1024]{2,1,0:T(2,128)(2,1)} %slice_bitcast_fusion.10), calls=%async_computation.2 | async-start | bytes 65536 | tf_op jit(solution)/shard_map/all_to_all | solution.py:82
  339.8 18.6 %all-to-all-start = ((bf16[8,2,1024]{2,1,0:T(2,128)(2,1)}), bf16[8,2,1024]{2,1,0:T(2,128)(2,1)S(1)}, u32[]{:S(2)}, u32[]{:S(2)}) async-start(bf16[8,2,1024]{2,1,0:T(2,128)(2,1)} %slice_bitcast_fusion.11), calls=%async_computation | async-start | bytes 65536 | tf_op jit(solution)/shard_map/all_to_all | solution.py:82
  429.6 5.8 %copy-start.16 = (f32[32,2,1023]{2,1,0:T(2,128)S(1)}, f32[32,2,1023]{2,1,0:T(2,128)}, u32[]{:S(2)}) copy-start(f32[32,2,1023]{2,1,0:T(2,128)} %slice.397) | copy-start | bytes 785668
  447.7 6.4 %copy-start.2 = (f32[32,2,4096]{2,0,1:T(8,128)S(1)}, f32[32,2,4096]{2,0,1:T(8,128)}, u32[]{:S(2)}) copy-start(f32[32,2,4096]{2,0,1:T(8,128)} %copy.121) | copy-start | bytes 3145732
  447.8 6.4 %copy-start.3 = (f32[32,2,4096]{2,0,1:T(8,128)S(1)}, f32[32,2,4096]{2,0,1:T(8,128)}, u32[]{:S(2)}) copy-start(f32[32,2,4096]{2,0,1:T(8,128)} %copy.115) | copy-start | bytes 3145732
  450.4 5.3 %copy-start.22 = (f32[4096]{0:T(1024)S(1)}, f32[4096]{0:T(1024)}, u32[]{:S(2)}) copy-start(f32[4096]{0:T(1024)} %mul.561) | copy-start | bytes 49156
  450.5 5.3 %copy-start.23 = (f32[4096]{0:T(1024)S(1)}, f32[4096]{0:T(1024)}, u32[]{:S(2)}) copy-start(f32[4096]{0:T(1024)} %mul.564) | copy-start | bytes 49156
  450.5 5.6 %copy-start.4 = (f32[32,2,4096]{2,0,1:T(8,128)S(1)}, f32[32,2,4096]{2,0,1:T(8,128)}, u32[]{:S(2)}) copy-start(f32[32,2,4096]{2,0,1:T(8,128)} %copy.111) | copy-start | bytes 3145732
  454.2 1.9 copy-start.5
  454.2 1.9 copy-start.14
  454.2 1.9 copy-start.15
  455.7 2.4 copy-start.1
  455.7 1.7 copy-start.6
  455.7 2.0 copy-start.7
  455.8 2.1 copy-start.12
  455.8 2.2 copy-start.13
  456.3 2.1 copy-start.8
  456.3 2.3 copy-start.9
  456.3 2.4 copy-start.10
  456.4 2.6 copy-start.11
  459.1 14.4 %copy-start.20 = (bf16[1,64,128]{2,1,0:T(8,128)(2,1)S(1)}, bf16[1,64,128]{2,1,0:T(8,128)(2,1)}, u32[]{:S(2)}) copy-start(bf16[1,64,128]{2,1,0:T(8,128)(2,1)} %get-tuple-element.254) | copy-start | bytes 49156
  459.1 14.4 %copy-start.21 = (bf16[1,64,128]{2,1,0:T(8,128)(2,1)S(1)}, bf16[1,64,128]{2,1,0:T(8,128)(2,1)}, u32[]{:S(2)}) copy-start(bf16[1,64,128]{2,1,0:T(8,128)(2,1)} %get-tuple-element.255) | copy-start | bytes 49156
  (4 other events, 4.6 us)
where the time goes:
time: 484 us; the launch traced here: 478 us
  blocking collectives  199 us (41%)
  local copies, waits for them, and re-layouts  142 us (29%)
  matrix products  46 us (10%)
  starting transfers between devices  45.2 us (9%)
  other arithmetic  35.4 us (7%)
  between operations  11 us (2%)
    all_gather x4, blocking collectives, shards(): lax.all_gather(mine_pieces, 'pulse', axis=0, tiled=True)  53.7 us
    all_gather x4, blocking collectives, shards(): lax.all_gather(mine_edges, 'pulse', axis=0, tiled=True)  53.4 us
    gather x96, local copies, waits for them, and re-layouts  44.3 us
    all_gather x1, blocking collectives, shards(): lax.all_gather(pulse_order, ('pulse', 'tile'), axis=0, tiled=True)  42.3 us
    unnamed x1, blocking collectives  37.2 us
    all_to_all x4, starting transfers between devices, shards(): lax.all_to_all(edges, 'tile', split_axis=0, concat_axis=0, tiled=True)  28.5 us
    reduce_sum x4, other arithmetic, shards(): summed = jnp.sum(samples, axis=0)  20.3 us
    all_to_all x4, starting transfers between devices, shards(): lax.all_to_all(pieces, 'tile', split_axis=0, concat_axis=0, tiled=True)  16.7 us
  transfers between devices with their start and end apart: 8, of which 0 were waited for; matrix products, arithmetic and copies ran while one was open for 22% of the time, Pallas kernels for 0%

commit v1 on v0

--- a/solution.py
+++ b/solution.py
@@ -7,6 +7,16 @@
 STEPS = 4
 PS = 1
 R_DEV = 128
+
+
+def gather_around(x, axis, dim):
+    ways, here, turn = (lax.axis_size(axis), lax.axis_index(axis), x.shape[dim])
+    shape = [n * ways if d == dim else n for d, n in enumerate(x.shape)]
+    full = lax.dynamic_update_slice_in_dim(jnp.zeros(shape, x.dtype), x, here * turn, axis=dim)
+    for far in range(1, ways):
+        x = lax.ppermute(x, axis, [(d, (d + 1) % ways) for d in range(ways)])
+        full = lax.dynamic_update_slice_in_dim(full, x, (here - far) % ways * turn, axis=dim)
+    return full
 
 
 def compress(windows, filt):
@@ -84,7 +94,7 @@
         )
         pieces, edges = (
             lax.all_gather(mine_pieces, "pulse", axis=0, tiled=True),
-            lax.all_gather(mine_edges, "pulse", axis=0, tiled=True),
+            gather_around(mine_edges, "pulse", 0),
         )
         shifts = jnp.take(all_fine, chosen)
         samples = interpolate(pieces, edges, shifts)

time: 484 us -> 462 us (0.955)
  blocking collectives: 199 us -> 145 us
  starting transfers between devices: 45.2 us -> 65 us
  waiting for transfers between devices: 0.02 us -> 11.9 us
    all_gather x4 -> x0, blocking collectives: 53.4 us -> none  [shards(): lax.all_gather(mine_edges, 'pulse', axis=0, tiled=True)]
    ppermute x0 -> x12, starting transfers between devices: none -> 21.4 us  [gather_around(): x = lax.ppermute(x, axis, [(d, (d + 1) % ways) for d in range(ways)])]
    ppermute x0 -> x12, waiting for transfers between devices: none -> 7.12 us  [gather_around(): x = lax.ppermute(x, axis, [(d, (d + 1) % ways) for d in range(ways)])]
  transfers between devices with their start and end apart: 8 -> 20, of which waited for: 0 -> 11; matrix products, arithmetic and copies ran while one was open for 22% -> 23% of each run, Pallas kernels for 0% -> 0%
where the time goes in v1:
time: 462 us; the launch traced here: 456 us
  blocking collectives  145 us (31%)
  local copies, waits for them, and re-layouts  141 us (31%)
  starting transfers between devices  65 us (14%)
  matrix products  46 us (10%)
  other arithmetic  35.5 us (8%)
  waiting for transfers between devices  11.9 us (3%)
  between operations  11.5 us (2%)
    all_gather x4, blocking collectives, shards(): lax.all_gather(mine_pieces, 'pulse', axis=0, tiled=True)  53.5 us
    gather x96, local copies, waits for them, and re-layouts  42.5 us
    all_gather x1, blocking collectives, shards(): lax.all_gather(pulse_order, ('pulse', 'tile'), axis=0, tiled=True)  42.3 us
    unnamed x1, blocking collectives  37.2 us
    all_to_all x4, starting transfers between devices, shards(): lax.all_to_all(edges, 'tile', split_axis=0, concat_axis=0, tiled=True)  27.8 us
    ppermute x12, starting transfers between devices, gather_around(): x = lax.ppermute(x, axis, [(d, (d + 1) % ways) for d in range(ways)])  21.4 us
    reduce_sum x4, other arithmetic, shards(): summed = jnp.sum(samples, axis=0)  20.3 us
    all_to_all x4, starting transfers between devices, shards(): lax.all_to_all(pieces, 'tile', split_axis=0, concat_axis=0, tiled=True)  15.7 us
  transfers between devices with their start and end apart: 20, of which 11 were waited for; matrix products, arithmetic and copies ran while one was open for 23% of the time, Pallas kernels for 0%

profile of v1, /device:TPU:0, one launch (start us, length us, event | category | flops | bytes accessed | tf_op | source)
XLA Modules:
  0.0 456.2 jit_solution(14577719925633564894)
XLA Ops:
  17.2 3.3 fusion.19
  22.1 10.5 %while.17 = (s32[]{:T(128)}, bf16[1,2,2048]{2,1,0:T(2,128)(2,1)S(1)}, s32[8,3]{0,1:T(4,128)S(1)}, bf16[8,2,1025]{2,1,0:T(2,128)(2,1)S(1)}, s32[]{:T(128)}) while((s32[]{:T(128)}, bf16[1,2,2048]{2,1,0:T(2,128)(2,1)S(1)}, s32[8,3]{0,1:T(4,128)S(1)}, bf16[8,2,1025]{2,1,0:T(2,128)(2,1)S(1)}, s32[]{:T(128)}) %tuple.191), condition=%wide.while_cond.13, body=%wide.while_body.13.sunk | while | flops 2 | bytes 9321 | solution.py:35
  33.4 5.2 %all-to-all-start.7 = ((bf16[8,1,2]{2,1,0:T(2,128)(2,1)}), bf16[8,1,2]{2,1,0:T(2,128)(2,1)S(1)}, u32[]{:S(2)}, u32[]{:S(2)}) async-start(bf16[8,1,2]{2,1,0:T(2,128)(2,1)} %copy.169), calls=%async_computation.7 | async-start | bytes 8192 | tf_op jit(solution)/shard_map/all_to_all | solution.py:93
  39.2 42.3 %all-gather = s32[32,1,4]{2,1,0:T(1,128)S(1)} all-gather(s32[1,1,4]{2,1,0:T(1,128)S(1)} %bitcast.340), channel_id=1, replica_groups=mesh['pulse'=4,'tile'=8] {'pulse','tile'}, dimensions={0}, use_global_device_ids=true | all-gather | bytes 528 | tf_op jit(solution)/shard_map/all_gather | solution.py:69
  82.1 37.2 %all-reduce.6 = (s32[128]{0:T(128)S(1)}, s32[128]{0:T(128)S(1)}) all-reduce(s32[128]{0:T(128)S(1)} %dynamic-update-slice.19, s32[128]{0:T(128)S(1)} %dynamic-update-slice.18), channel_id=1, replica_groups=mesh['pulse'=4,'tile'=8] {'pulse','tile'}, use_global_device_ids=true, to_apply=%add.5 | all-reduce | flops 256 | bytes 2048
  136.5 10.5 %while.16 = (s32[]{:T(128)}, bf16[1,2,2048]{2,1,0:T(2,128)(2,1)S(1)}, s32[8,3]{0,1:T(4,128)S(1)}, bf16[8,2,1025]{2,1,0:T(2,128)(2,1)S(1)}, s32[]{:T(128)}) while((s32[]{:T(128)}, bf16[1,2,2048]{2,1,0:T(2,128)(2,1)S(1)}, s32[8,3]{0,1:T(4,128)S(1)}, bf16[8,2,1025]{2,1,0:T(2,128)(2,1)S(1)}, s32[]{:T(128)}) %tuple.188), condition=%wide.while_cond.10, body=%wide.while_body.10.sunk | while | flops 2 | bytes 9321 | solution.py:35
  159.1 10.8 %while.15 = (s32[]{:T(128)}, bf16[1,2,2048]{2,1,0:T(2,128)(2,1)S(1)}, s32[8,3]{0,1:T(4,128)S(1)}, bf16[8,2,1025]{2,1,0:T(2,128)(2,1)S(1)}, s32[]{:T(128)}) while((s32[]{:T(128)}, bf16[1,2,2048]{2,1,0:T(2,128)(2,1)S(1)}, s32[8,3]{0,1:T(4,128)S(1)}, bf16[8,2,1025]{2,1,0:T(2,128)(2,1)S(1)}, s32[]{:T(128)}) %tuple.185), condition=%wide.while_cond.7, body=%wide.while_body.7.sunk | while | flops 2 | bytes 9321 | solution.py:35
  182.0 10.8 %while.14 = (s32[]{:T(128)}, bf16[1,2,2048]{2,1,0:T(2,128)(2,1)S(1)}, s32[8,3]{0,1:T(4,128)S(1)}, bf16[8,2,1025]{2,1,0:T(2,128)(2,1)S(1)}, s32[]{:T(128)}) while((s32[]{:T(128)}, bf16[1,2,2048]{2,1,0:T(2,128)(2,1)S(1)}, s32[8,3]{0,1:T(4,128)S(1)}, bf16[8,2,1025]{2,1,0:T(2,128)(2,1)S(1)}, s32[]{:T(128)}) %tuple.182), condition=%wide.while_cond.4, body=%wide.while_body.4.sunk | while | flops 2 | bytes 9321 | solution.py:35
  217.9 16.0 %all-to-all-start.5 = ((bf16[8,1,2]{2,1,0:T(2,128)(2,1)}), bf16[8,1,2]{2,1,0:T(2,128)(2,1)S(1)}, u32[]{:S(2)}, u32[]{:S(2)}) async-start(bf16[8,1,2]{2,1,0:T(2,128)(2,1)} %copy.155), calls=%async_computation.5 | async-start | bytes 8192 | tf_op jit(solution)/shard_map/all_to_all | solution.py:93
  246.5 3.3 all-to-all-start.1
  279.6 4.1 all-to-all-start.4
  283.8 13.4 %all_gather.27 = bf16[32,2,1024]{2,1,0:T(2,128)(2,1)S(1)} all-gather(bf16[8,2,1024]{2,1,0:T(2,128)(2,1)S(1)} %all-to-all-done.6), channel_id=1, replica_groups=mesh['pulse'=4,'tile'=8] {'pulse'}, dimensions={0}, use_global_device_ids=true | all-gather | bytes 163840 | tf_op jit(solution)/shard_map/all_gather | solution.py:96
  298.7 4.1 all-to-all-start.2
  302.7 13.4 %all_gather.26 = bf16[32,2,1024]{2,1,0:T(2,128)(2,1)S(1)} all-gather(bf16[8,2,1024]{2,1,0:T(2,128)(2,1)S(1)} %all-to-all-done.4), channel_id=1, replica_groups=mesh['pulse'=4,'tile'=8] {'pulse'}, dimensions={0}, use_global_device_ids=true | all-gather | bytes 163840 | tf_op jit(solution)/shard_map/all_gather | solution.py:96
  318.2 4.2 all-to-all-start
  322.4 13.4 %all_gather.25 = bf16[32,2,1024]{2,1,0:T(2,128)(2,1)S(1)} all-gather(bf16[8,2,1024]{2,1,0:T(2,128)(2,1)S(1)} %all-to-all-done.2), channel_id=1, replica_groups=mesh['pulse'=4,'tile'=8] {'pulse'}, dimensions={0}, use_global_device_ids=true | all-gather | bytes 163840 | tf_op jit(solution)/shard_map/all_gather | solution.py:96
  336.9 13.4 %all_gather.23 = bf16[32,2,1024]{2,1,0:T(2,128)(2,1)S(1)} all-gather(bf16[8,2,1024]{2,1,0:T(2,128)(2,1)S(1)} %all-to-all-done), channel_id=1, replica_groups=mesh['pulse'=4,'tile'=8] {'pulse'}, dimensions={0}, use_global_device_ids=true | all-gather | bytes 163840 | tf_op jit(solution)/shard_map/all_gather | solution.py:96
  354.6 3.6 copy.177
  358.2 3.9 broadcast_in_dim.195
  362.1 3.6 copy.167
  365.7 5.1 %add_reduce_fusion = f32[2,1024,4]{2,1,0:T(8,128)S(1)} fusion(f32[32,1024,4]{0,2,1:T(4,128)} %copy.179, f32[32,1024,4]{0,2,1:T(4,128)} %copy.178, f32[32,2,1024]{0,2,1:T(8,128)S(1)} %copy.176, f32[32,2,1024]{0,2,1:T(8,128)} %copy.166), kind=kLoop, calls=%fused_computation.52 | loop fusion | flops 1040384 | bytes 1605632 | tf_op jit(solution)/shard_map/reduce_sum | solution.py:101
  376.8 3.6 copy.163
  380.4 3.9 broadcast_in_dim.185
  384.4 3.6 copy.153
  388.0 5.1 %add_reduce_fusion.1 = f32[2,1024,4]{2,1,0:T(8,128)S(1)} fusion(f32[32,1024,4]{0,2,1:T(4,128)} %copy.165, f32[32,1024,4]{0,2,1:T(4,128)} %copy.164, f32[32,2,1024]{0,2,1:T(8,128)S(1)} %copy.162, f32[32,2,1024]{0,2,1:T(8,128)} %copy.152), kind=kLoop, calls=%fused_computation.53 | loop fusion | flops 1040384 | bytes 1605632 | tf_op jit(solution)/shard_map/reduce_sum | solution.py:101
  397.8 3.6 copy.149
  404.1 3.6 copy.139
  407.7 5.1 %add_reduce_fusion.2 = f32[2,1024,4]{2,1,0:T(8,128)S(1)} fusion(f32[32,1024,4]{0,2,1:T(4,128)} %copy.151, f32[32,1024,4]{0,2,1:T(4,128)} %copy.150, f32[32,2,1024]{0,2,1:T(8,128)S(1)} %copy.148, f32[32,2,1024]{0,2,1:T(8,128)S(1)} %copy.138), kind=kLoop, calls=%fused_computation.54 | loop fusion | flops 1040384 | bytes 1605632 | tf_op jit(solution)/shard_map/reduce_sum | solution.py:101
  414.0 5.0 %add_reduce_fusion.3 = f32[2,1024,4]{2,1,0:T(8,128)S(1)} fusion(f32[32,1024,4]{0,2,1:T(4,128)} %copy.137, f32[32,1024,4]{0,2,1:T(4,128)} %copy.136, f32[32,2,1024]{0,2,1:T(8,128)S(1)} %copy.134, f32[32,2,1024]{0,2,1:T(8,128)S(1)} %copy.124), kind=kLoop, calls=%fused_computation.55 | loop fusion | flops 1040384 | bytes 1605632 | tf_op jit(solution)/shard_map/reduce_sum | solution.py:101
  422.3 3.6 copy.135
  428.6 3.7 copy.125
  437.5 12.1 %all-reduce.7 = (f32[32]{0:T(128)S(1)}, f32[32]{0:T(128)S(1)}, f32[32]{0:T(128)S(1)}, f32[32]{0:T(128)S(1)}, f32[32]{0:T(128)S(1)}, /*index=5*/f32[32]{0:T(128)S(1)}, f32[32]{0:T(128)S(1)}, f32[32]{0:T(128)S(1)}) all-reduce(f32[32]{0:T(128)S(1)} %get-tuple-element.157, ...), channel_id=1, replica_groups=mesh['pulse'=4,'tile'=8] {'tile'}, use_global_device_ids=true, to_apply=%region_4.8 | all-reduce | flops 256 | bytes 2048 | tf_op jit(solution)/shard_map/psum | solution.py:103
  (386 shorter events, 202.1 us)
Async XLA Ops:
  14.2 6.3 %copy-start = (bf16[2,1024,2048]{2,1,0:T(8,128)(2,1)S(1)}, bf16[2,1024,2048]{2,1,0:T(8,128)(2,1)}, u32[]{:S(2)}) copy-start(bf16[2,1024,2048]{2,1,0:T(8,128)(2,1)} %param.14) | copy-start | bytes 25165828
  20.6 18.6 %copy-start.24 = (s32[1,4]{1,0:T(1,128)S(1)}, s32[1,4]{1,0:T(1,128)}, u32[]{:S(2)}) copy-start(s32[1,4]{1,0:T(1,128)} %param.18) | copy-start | bytes 52
  20.6 61.0 %copy-start.26 = (s32[4]{0:T(128)S(1)}, s32[4]{0:T(128)}, u32[]{:S(2)}) copy-start(s32[4]{0:T(128)} %param.17) | copy-start | bytes 52
  20.6 61.2 %copy-start.27 = (s32[4]{0:T(128)S(1)}, s32[4]{0:T(128)}, u32[]{:S(2)}) copy-start(s32[4]{0:T(128)} %param.16) | copy-start | bytes 52
  33.4 184.5 %all-to-all-start.7 = ((bf16[8,1,2]{2,1,0:T(2,128)(2,1)}), bf16[8,1,2]{2,1,0:T(2,128)(2,1)S(1)}, u32[]{:S(2)}, u32[]{:S(2)}) async-start(bf16[8,1,2]{2,1,0:T(2,128)(2,1)} %copy.169), calls=%async_computation.7 | async-start | bytes 8192 | tf_op jit(solution)/shard_map/all_to_all | solution.py:93
  217.9 20.7 %all-to-all-start.5 = ((bf16[8,1,2]{2,1,0:T(2,128)(2,1)}), bf16[8,1,2]{2,1,0:T(2,128)(2,1)S(1)}, u32[]{:S(2)}, u32[]{:S(2)}) async-start(bf16[8,1,2]{2,1,0:T(2,128)(2,1)} %copy.155), calls=%async_computation.5 | async-start | bytes 8192 | tf_op jit(solution)/shard_map/all_to_all | solution.py:93
  234.1 26.9 %collective-permute-start.9 = (bf16[8,2]{0,1:T(2,128)(2,1)S(1)}, bf16[8,2]{0,1:T(2,128)(2,1)S(1)}, u32[]{:S(2)}, u32[]{:S(2)}) collective-permute-start(bf16[8,2]{0,1:T(2,128)(2,1)S(1)} %bitcast.343), channel_id=1, source_target_pairs={{0,8},{8,16},{16,24},{24,0},{1,9},{9,17},{17,25},{25,1},{2,10},{10... | collective-permute-start | bytes 104 | tf_op jit(solution)/shard_map/ppermute | solution.py:17
  238.6 7.9 %all-to-all-start.3 = ((bf16[8,1,2]{2,1,0:T(2,128)(2,1)}), bf16[8,1,2]{2,1,0:T(2,128)(2,1)S(1)}, u32[]{:S(2)}, u32[]{:S(2)}) async-start(bf16[8,1,2]{2,1,0:T(2,128)(2,1)} %copy.141), calls=%async_computation.3 | async-start | bytes 8192 | tf_op jit(solution)/shard_map/all_to_all | solution.py:93
  242.1 19.0 %collective-permute-start.6 = (bf16[8,2]{0,1:T(2,128)(2,1)S(1)}, bf16[8,2]{0,1:T(2,128)(2,1)S(1)}, u32[]{:S(2)}, u32[]{:S(2)}) collective-permute-start(bf16[8,2]{0,1:T(2,128)(2,1)S(1)} %bitcast.345), channel_id=1, source_target_pairs={{0,8},{8,16},{16,24},{24,0},{1,9},{9,17},{17,25},{25,1},{2,10},{10... | collective-permute-start | bytes 104 | tf_op jit(solution)/shard_map/ppermute | solution.py:17
  246.5 8.0 %all-to-all-start.1 = ((bf16[8,1,2]{2,1,0:T(2,128)(2,1)}), bf16[8,1,2]{2,1,0:T(2,128)(2,1)S(1)}, u32[]{:S(2)}, u32[]{:S(2)}) async-start(bf16[8,1,2]{2,1,0:T(2,128)(2,1)} %copy.127), calls=%async_computation.1 | async-start | bytes 8192 | tf_op jit(solution)/shard_map/all_to_all | solution.py:93
  250.0 11.2 %collective-permute-start.3 = (bf16[8,2]{0,1:T(2,128)(2,1)S(1)}, bf16[8,2]{0,1:T(2,128)(2,1)S(1)}, u32[]{:S(2)}, u32[]{:S(2)}) collective-permute-start(bf16[8,2]{0,1:T(2,128)(2,1)S(1)} %bitcast.347), channel_id=1, source_target_pairs={{0,8},{8,16},{16,24},{24,0},{1,9},{9,17},{17,25},{25,1},{2,10},{10... | collective-permute-start | bytes 104 | tf_op jit(solution)/shard_map/ppermute | solution.py:17
  254.4 25.2 %all-to-all-start.6 = ((bf16[8,2,1024]{2,1,0:T(2,128)(2,1)}), bf16[8,2,1024]{2,1,0:T(2,128)(2,1)S(1)}, u32[]{:S(2)}, u32[]{:S(2)}) async-start(bf16[8,2,1024]{2,1,0:T(2,128)(2,1)} %slice_bitcast_fusion.8), calls=%async_computation.6 | async-start | bytes 65536 | tf_op jit(solution)/shard_map/all_to_all | solution.py:92
  258.0 5.4 %collective-permute-start = (bf16[8,2]{0,1:T(2,128)(2,1)S(1)}, bf16[8,2]{0,1:T(2,128)(2,1)S(1)}, u32[]{:S(2)}, u32[]{:S(2)}) collective-permute-start(bf16[8,2]{0,1:T(2,128)(2,1)S(1)} %bitcast.349), channel_id=1, source_target_pairs={{0,8},{8,16},{16,24},{24,0},{1,9},{9,17},{17,25},{25,1},{2,10},{10... | collective-permute-start | bytes 104 | tf_op jit(solution)/shard_map/ppermute | solution.py:17
  263.5 5.4 %collective-permute-start.10 = (bf16[8,2]{0,1:T(2,128)(2,1)S(1)}, bf16[8,2]{0,1:T(2,128)(2,1)S(1)}, u32[]{:S(2)}, u32[]{:S(2)}) collective-permute-start(bf16[8,2]{0,1:T(2,128)(2,1)S(1)} %collective-permute-done.9), channel_id=1, source_target_pairs={{0,8},{8,16},{16,24},{24,0},{1,9},{9,17},{17,25},{25,1},{2,10},{10... | collective-permute-start | bytes 104 | tf_op jit(solution)/shard_map/ppermute | solution.py:17
  264.6 5.4 %collective-permute-start.7 = (bf16[8,2]{0,1:T(2,128)(2,1)S(1)}, bf16[8,2]{0,1:T(2,128)(2,1)S(1)}, u32[]{:S(2)}, u32[]{:S(2)}) collective-permute-start(bf16[8,2]{0,1:T(2,128)(2,1)S(1)} %collective-permute-done.6), channel_id=1, source_target_pairs={{0,8},{8,16},{16,24},{24,0},{1,9},{9,17},{17,25},{25,1},{2,10},{10... | collective-permute-start | bytes 104 | tf_op jit(solution)/shard_map/ppermute | solution.py:17
  265.3 5.4 %collective-permute-start.4 = (bf16[8,2]{0,1:T(2,128)(2,1)S(1)}, bf16[8,2]{0,1:T(2,128)(2,1)S(1)}, u32[]{:S(2)}, u32[]{:S(2)}) collective-permute-start(bf16[8,2]{0,1:T(2,128)(2,1)S(1)} %collective-permute-done.3), channel_id=1, source_target_pairs={{0,8},{8,16},{16,24},{24,0},{1,9},{9,17},{17,25},{25,1},{2,10},{10... | collective-permute-start | bytes 104 | tf_op jit(solution)/shard_map/ppermute | solution.py:17
  265.3 5.5 %collective-permute-start.1 = (bf16[8,2]{0,1:T(2,128)(2,1)S(1)}, bf16[8,2]{0,1:T(2,128)(2,1)S(1)}, u32[]{:S(2)}, u32[]{:S(2)}) collective-permute-start(bf16[8,2]{0,1:T(2,128)(2,1)S(1)} %collective-permute-done), channel_id=1, source_target_pairs={{0,8},{8,16},{16,24},{24,0},{1,9},{9,17},{17,25},{25,1},{2,10},{10... | collective-permute-start | bytes 104 | tf_op jit(solution)/shard_map/ppermute | solution.py:17
  270.9 5.4 %collective-permute-start.11 = (bf16[8,2]{0,1:T(2,128)(2,1)S(1)}, bf16[8,2]{0,1:T(2,128)(2,1)S(1)}, u32[]{:S(2)}, u32[]{:S(2)}) collective-permute-start(bf16[8,2]{0,1:T(2,128)(2,1)S(1)} %collective-permute-done.10), channel_id=1, source_target_pairs={{0,8},{8,16},{16,24},{24,0},{1,9},{9,17},{17,25},{25,1},{2,10},{10... | collective-permute-start | bytes 104 | tf_op jit(solution)/shard_map/ppermute | solution.py:17
  272.3 5.4 %collective-permute-start.8 = (bf16[8,2]{0,1:T(2,128)(2,1)S(1)}, bf16[8,2]{0,1:T(2,128)(2,1)S(1)}, u32[]{:S(2)}, u32[]{:S(2)}) collective-permute-start(bf16[8,2]{0,1:T(2,128)(2,1)S(1)} %collective-permute-done.7), channel_id=1, source_target_pairs={{0,8},{8,16},{16,24},{24,0},{1,9},{9,17},{17,25},{25,1},{2,10},{10... | collective-permute-start | bytes 104 | tf_op jit(solution)/shard_map/ppermute | solution.py:17
  273.4 5.4 %collective-permute-start.5 = (bf16[8,2]{0,1:T(2,128)(2,1)S(1)}, bf16[8,2]{0,1:T(2,128)(2,1)S(1)}, u32[]{:S(2)}, u32[]{:S(2)}) collective-permute-start(bf16[8,2]{0,1:T(2,128)(2,1)S(1)} %collective-permute-done.4), channel_id=1, source_target_pairs={{0,8},{8,16},{16,24},{24,0},{1,9},{9,17},{17,25},{25,1},{2,10},{10... | collective-permute-start | bytes 104 | tf_op jit(solution)/shard_map/ppermute | solution.py:17
  274.0 5.4 %collective-permute-start.2 = (bf16[8,2]{0,1:T(2,128)(2,1)S(1)}, bf16[8,2]{0,1:T(2,128)(2,1)S(1)}, u32[]{:S(2)}, u32[]{:S(2)}) collective-permute-start(bf16[8,2]{0,1:T(2,128)(2,1)S(1)} %collective-permute-done.1), channel_id=1, source_target_pairs={{0,8},{8,16},{16,24},{24,0},{1,9},{9,17},{17,25},{25,1},{2,10},{10... | collective-permute-start | bytes 104 | tf_op jit(solution)/shard_map/ppermute | solution.py:17
  279.6 19.0 %all-to-all-start.4 = ((bf16[8,2,1024]{2,1,0:T(2,128)(2,1)}), bf16[8,2,1024]{2,1,0:T(2,128)(2,1)S(1)}, u32[]{:S(2)}, u32[]{:S(2)}) async-start(bf16[8,2,1024]{2,1,0:T(2,128)(2,1)} %slice_bitcast_fusion.9), calls=%async_computation.4 | async-start | bytes 65536 | tf_op jit(solution)/shard_map/all_to_all | solution.py:92
  298.7 19.6 %all-to-all-start.2 = ((bf16[8,2,1024]{2,1,0:T(2,128)(2,1)}), bf16[8,2,1024]{2,1,0:T(2,128)(2,1)S(1)}, u32[]{:S(2)}, u32[]{:S(2)}) async-start(bf16[8,2,1024]{2,1,0:T(2,128)(2,1)} %slice_bitcast_fusion.10), calls=%async_computation.2 | async-start | bytes 65536 | tf_op jit(solution)/shard_map/all_to_all | solution.py:92
  318.2 18.7 %all-to-all-start = ((bf16[8,2,1024]{2,1,0:T(2,128)(2,1)}), bf16[8,2,1024]{2,1,0:T(2,128)(2,1)S(1)}, u32[]{:S(2)}, u32[]{:S(2)}) async-start(bf16[8,2,1024]{2,1,0:T(2,128)(2,1)} %slice_bitcast_fusion.11), calls=%async_computation | async-start | bytes 65536 | tf_op jit(solution)/shard_map/all_to_all | solution.py:92
  407.7 5.8 %copy-start.16 = (f32[32,2,1023]{2,1,0:T(2,128)S(1)}, f32[32,2,1023]{2,1,0:T(2,128)}, u32[]{:S(2)}) copy-start(f32[32,2,1023]{2,1,0:T(2,128)} %slice.397) | copy-start | bytes 785668
  425.9 6.4 %copy-start.2 = (f32[32,2,4096]{2,0,1:T(8,128)S(1)}, f32[32,2,4096]{2,0,1:T(8,128)}, u32[]{:S(2)}) copy-start(f32[32,2,4096]{2,0,1:T(8,128)} %copy.177) | copy-start | bytes 3145732
  425.9 6.4 %copy-start.3 = (f32[32,2,4096]{2,0,1:T(8,128)S(1)}, f32[32,2,4096]{2,0,1:T(8,128)}, u32[]{:S(2)}) copy-start(f32[32,2,4096]{2,0,1:T(8,128)} %copy.167) | copy-start | bytes 3145732
  428.6 5.2 %copy-start.22 = (f32[4096]{0:T(1024)S(1)}, f32[4096]{0:T(1024)}, u32[]{:S(2)}) copy-start(f32[4096]{0:T(1024)} %mul.589) | copy-start | bytes 49156
  428.6 5.2 %copy-start.23 = (f32[4096]{0:T(1024)S(1)}, f32[4096]{0:T(1024)}, u32[]{:S(2)}) copy-start(f32[4096]{0:T(1024)} %mul.592) | copy-start | bytes 49156
  428.6 5.6 %copy-start.4 = (f32[32,2,4096]{2,0,1:T(8,128)S(1)}, f32[32,2,4096]{2,0,1:T(8,128)}, u32[]{:S(2)}) copy-start(f32[32,2,4096]{2,0,1:T(8,128)} %copy.163) | copy-start | bytes 3145732
  437.2 14.4 %copy-start.20 = (bf16[1,64,128]{2,1,0:T(8,128)(2,1)S(1)}, bf16[1,64,128]{2,1,0:T(8,128)(2,1)}, u32[]{:S(2)}) copy-start(bf16[1,64,128]{2,1,0:T(8,128)(2,1)} %get-tuple-element.254) | copy-start | bytes 49156
  437.2 14.4 %copy-start.21 = (bf16[1,64,128]{2,1,0:T(8,128)(2,1)S(1)}, bf16[1,64,128]{2,1,0:T(8,128)(2,1)}, u32[]{:S(2)}) copy-start(bf16[1,64,128]{2,1,0:T(8,128)(2,1)} %get-tuple-element.255) | copy-start | bytes 49156
  (16 other events, 30.1 us)
